TPU v7x, 768 devices: a whole 4x8x12 slice. The times are simulated.
768 devices in a mesh: segment: 24 (over z, core), expert: 32 (over y, x).
Axes of the slice: x: 4, y: 8, z: 12, core: 2. Of those that a mesh axis runs over, the one named last changes fastest.
Arguments:
- hidden: bfloat16 [24, 2048, 4096], P('segment', 'expert'), may hold values from -6 to 6
- expert_ids: int32 [2, 24, 2048, 8], P(None, 'segment', 'expert'), may hold values from 0 to 127, as said below
- route_weights: float32 [2, 24, 2048, 8], P(None, 'segment', 'expert'), may hold values from 0.2 to 1
- norm_gain: bfloat16 [24, 4096], P('segment'), may hold values from 0.099609375 to 1.8984375
- w_gate: bfloat16 [24, 4096, 4096], P('segment', None, 'expert'), may hold values from -0.09375 to 0.09375
- w_up: bfloat16 [24, 4096, 4096], P('segment', None, 'expert'), may hold values from -0.09375 to 0.09375
- w_down: bfloat16 [24, 4096, 4096], P('segment', 'expert'), may hold values from -0.1875 to 0.1875
Outputs:
- handed: bfloat16 [24, 2048, 4096], P('segment', 'expert')
Inputs may be any that keep to these rules, and one draw needn't show every extreme that they name: `expert_ids`: each row names 8 different experts. In each aligned block of 64 rows (the rows of one device) each of the experts 0 .. 3 is named by at most 8 rows, and some expert of them by exactly 8 rows in every block.
All inputs are finite; a program needn't handle non-finite values.
Results may differ from a plain program's by a relative error of at most 0.0034.
Values may be sent and summed in bfloat16 or wider, within the bound.
A program may use at most 32 MiB of HBM per device.

v0:
```python
import jax
import jax.numpy as jnp
from jax import lax
from jax.sharding import PartitionSpec as P

SLICES = 8
MOST = 8
TICKS = 2


EPS = 1e-06


def passed_along(value, axis, steps):
    count = lax.axis_size(axis)
    pairs = [(source, (source + steps) % count) for source in range(count)]
    return lax.ppermute(value, axis, pairs)


def expert_rows(taken_rows, w_gate, w_up, w_down):
    gate_out = jnp.einsum("snd,df->snf", taken_rows, w_gate, preferred_element_type=jnp.float32)
    up_out = jnp.einsum("snd,df->snf", taken_rows, w_up, preferred_element_type=jnp.float32)
    active = (jax.nn.silu(gate_out) * up_out).astype(jnp.bfloat16)
    return jnp.einsum("snf,fd->snd", active, w_down, preferred_element_type=jnp.float32).astype(
        jnp.bfloat16
    )


def moe_layer(current, route_ids, route_weight, gain_row, w_gate, w_up, w_down, capacity, slices):
    rows_here, model_width = current.shape
    devices = lax.axis_size("expert")
    experts_here = devices // slices
    widened = current.astype(jnp.float32)
    normed = (
        widened
        * lax.rsqrt(jnp.mean(widened * widened, axis=-1, keepdims=True) + EPS)
        * gain_row.astype(jnp.float32)
    ).astype(jnp.bfloat16)
    matches = route_ids[:, :, None] == jnp.arange(experts_here, dtype=jnp.int32)[None, None, :]
    members = jnp.any(matches, axis=1)
    route_share = jnp.sum(jnp.where(matches, route_weight[:, :, None], jnp.float32(0.0)), axis=1)
    slot_rank = jnp.cumsum(members.astype(jnp.int32), axis=0) - 1
    placement = members[:, :, None] & (
        slot_rank[:, :, None] == jnp.arange(capacity, dtype=jnp.int32)[None, None, :]
    )
    packed = jnp.einsum(
        "rec,rd->ecd", placement.astype(jnp.bfloat16), normed, preferred_element_type=jnp.float32
    ).astype(jnp.bfloat16)
    copies = jnp.broadcast_to(
        packed[:, None], (experts_here, slices, capacity, model_width)
    ).reshape(devices, capacity, model_width)
    partial_value = expert_rows(
        lax.all_to_all(copies, "expert", split_axis=0, concat_axis=0, tiled=True),
        w_gate,
        w_up,
        w_down,
    )
    returned = lax.all_to_all(partial_value, "expert", split_axis=0, concat_axis=0, tiled=True)
    totals = jnp.sum(
        returned.reshape(experts_here, slices, capacity, model_width).astype(jnp.float32), axis=1
    )
    weight_slots = jnp.where(placement, route_share[:, :, None], jnp.float32(0.0))
    branch = jnp.einsum("rec,ecd->rd", weight_slots, totals, precision=lax.Precision.HIGHEST)
    return (widened + branch).astype(jnp.bfloat16)


def body(hidden, expert_ids, route_weights, norm_gain, w_gate, w_up, w_down):
    current = hidden[0]
    for tick_index in range(TICKS):
        result = moe_layer(
            current,
            expert_ids[tick_index, 0],
            route_weights[tick_index, 0],
            norm_gain[0],
            w_gate[0],
            w_up[0],
            w_down[0],
            MOST,
            SLICES,
        )
        current = passed_along(result, "segment", 1)
    return current[None]


def solution(mesh):
    return jax.shard_map(
        body,
        mesh=mesh,
        in_specs=(
            P("segment", "expert", None),
            P(None, "segment", "expert", None),
            P(None, "segment", "expert", None),
            P("segment", None),
            P("segment", None, "expert"),
            P("segment", None, "expert"),
            P("segment", "expert", None),
        ),
        out_specs=P("segment", "expert", None),
        check_vma=False,
    )
```

profile of v0, /device:TPU:145, one launch (start us, length us, event | category | flops | bytes accessed | tf_op | source)
XLA Modules:
  0.0 268.0 jit_solution(14568855099133506311)
XLA Ops:
  0.0 0.0 copy-start
  0.0 1.3 fusion.9
  1.4 0.7 slice_bitcast_fusion.1
  2.1 0.7 mul.69
  2.8 0.1 copy.16
  2.9 0.1 reduce_window_sum.17
  3.0 0.1 copy.17
  3.1 1.4 convolution_convert_fusion.3
  4.5 0.2 broadcast_in_dim.74
  4.7 0.0 copy-start.1
  4.7 58.9 %all_to_all.20 = bf16[32,8,4096]{2,1,0:T(8,128)(2,1)S(1)} all-to-all(bf16[32,8,4096]{2,1,0:T(8,128)(2,1)S(1)} %bitcast.70), channel_id=1, replica_groups=mesh['segment'=24,'expert'=32] {'expert'}, dimensions={0} | all-to-all | bytes 4194304 | tf_op jit(solution)/shard_map/all_to_all | solution.py:53
  63.6 0.0 copy-done.1
  63.6 0.7 fusion.20
  64.3 0.0 copy-done
  64.3 4.9 %convolution_convert_fusion.1 = bf16[32,8,4096]{2,1,0:T(8,128)(2,1)} fusion(bf16[32,8,4096]{2,1,0:T(8,128)(2,1)S(1)} %all_to_all.20, bf16[1,128,4096]{2,1,0:T(8,128)(2,1)S(1)} %copy-done, bf16[1,4096,128]{2,1,0:T(8,128)(2,1)} %param.12, f32[32,8,128]{2,1,0:T(8,128)S(1)} %fusion.20), kind=kOutput, calls=%fused_computation.1 | convolution fusion | flops 538116096 | bytes 6422528 | tf_op jit(solution)/shard_map/snf,fd->snd/dot_general | solution.py:24
  69.3 0.0 copy-start.6
  69.3 5.8 %all-to-all-start.1 = ((bf16[32,8,4096]{2,1,0:T(8,128)(2,1)}), bf16[32,8,4096]{2,1,0:T(8,128)(2,1)S(1)}, u32[]{:S(2)}, u32[]{:S(2)}) async-start(bf16[32,8,4096]{2,1,0:T(8,128)(2,1)} %convolution_convert_fusion.1), calls=%async_computation.1 | async-start | bytes 4194304 | tf_op jit(solution)/shard_map/all_to_all | solution.py:58
  75.0 0.0 copy-done.6
  75.1 47.8 %all-to-all-done.1 = bf16[32,8,4096]{2,1,0:T(8,128)(2,1)S(1)} async-done(((bf16[32,8,4096]{2,1,0:T(8,128)(2,1)}), bf16[32,8,4096]{2,1,0:T(8,128)(2,1)S(1)}, u32[]{:S(2)}, u32[]{:S(2)}) %all-to-all-start.1) | async-done | bytes 2097184 | tf_op jit(solution)/shard_map/all_to_all | solution.py:58
  122.9 0.0 copy-start.3
  122.9 0.3 convert_reduce_fusion.1
  123.2 0.7 copy-done.3
  123.9 1.1 fusion.3
  125.0 5.5 %collective-permute-start = (bf16[64,4096]{1,0:T(8,128)(2,1)S(1)}, bf16[64,4096]{1,0:T(8,128)(2,1)S(1)}, u32[]{:S(2)}, u32[]{:S(2)}) collective-permute-start(bf16[64,4096]{1,0:T(8,128)(2,1)S(1)} %fusion.3), channel_id=1, source_target_pairs={{0,32},{32,64},{64,96},{96,128},{128,160},{160,192},{192,224},{224... | collective-permute-start | bytes 1572872 | tf_op jit(solution)/shard_map/ppermute | solution.py:17
  130.6 0.1 copy.18
  130.7 0.1 reduce_window_sum.18
  130.8 0.1 copy.19
  130.8 5.8 %collective-permute-done = bf16[64,4096]{1,0:T(8,128)(2,1)S(1)} collective-permute-done((bf16[64,4096]{1,0:T(8,128)(2,1)S(1)}, bf16[64,4096]{1,0:T(8,128)(2,1)S(1)}, u32[]{:S(2)}, u32[]{:S(2)}) %collective-permute-start) | collective-permute-done | bytes 524320 | tf_op jit(solution)/shard_map/ppermute | solution.py:17
  136.7 0.0 copy-start.4
  136.7 0.2 fusion.6
  136.9 0.3 convolution_convert_fusion.2
  137.2 0.2 broadcast_in_dim.78
  137.5 0.0 copy-done.4
  137.5 0.0 copy-start.2
  137.5 54.9 %all_to_all.21 = bf16[32,8,4096]{2,1,0:T(8,128)(2,1)S(1)} all-to-all(bf16[32,8,4096]{2,1,0:T(8,128)(2,1)S(1)} %bitcast.71), channel_id=1, replica_groups=mesh['segment'=24,'expert'=32] {'expert'}, dimensions={0} | all-to-all | bytes 4194304 | tf_op jit(solution)/shard_map/all_to_all | solution.py:53
  192.4 0.0 copy-done.2
  192.4 0.7 fusion.18
  193.1 4.9 %convolution_convert_fusion = bf16[32,8,4096]{2,1,0:T(8,128)(2,1)} fusion(bf16[32,8,4096]{2,1,0:T(8,128)(2,1)S(1)} %all_to_all.21, bf16[1,128,4096]{2,1,0:T(8,128)(2,1)S(1)} %copy-done, bf16[1,4096,128]{2,1,0:T(8,128)(2,1)} %param.12, f32[32,8,128]{2,1,0:T(8,128)S(1)} %fusion.18), kind=kOutput, calls=%fused_computation | convolution fusion | flops 538116096 | bytes 6422528 | tf_op jit(solution)/shard_map/snf,fd->snd/dot_general | solution.py:24
  198.1 5.4 %all-to-all-start.3 = ((bf16[32,8,4096]{2,1,0:T(8,128)(2,1)}), bf16[32,8,4096]{2,1,0:T(8,128)(2,1)S(1)}, u32[]{:S(2)}, u32[]{:S(2)}) async-start(bf16[32,8,4096]{2,1,0:T(8,128)(2,1)} %convolution_convert_fusion), calls=%async_computation.3 | async-start | bytes 4194304 | tf_op jit(solution)/shard_map/all_to_all | solution.py:58
  203.5 47.9 %all-to-all-done.3 = bf16[32,8,4096]{2,1,0:T(8,128)(2,1)S(1)} async-done(((bf16[32,8,4096]{2,1,0:T(8,128)(2,1)}), bf16[32,8,4096]{2,1,0:T(8,128)(2,1)S(1)}, u32[]{:S(2)}, u32[]{:S(2)}) %all-to-all-start.3) | async-done | bytes 2097184 | tf_op jit(solution)/shard_map/all_to_all | solution.py:58
  251.4 0.0 copy-start.5
  251.4 0.3 convert_reduce_fusion
  251.7 0.7 copy-done.5
  252.4 1.1 fusion.2
  253.5 7.6 %collective-permute-start.1 = (bf16[64,4096]{1,0:T(8,128)(2,1)S(1)}, bf16[64,4096]{1,0:T(8,128)(2,1)S(1)}, u32[]{:S(2)}, u32[]{:S(2)}) collective-permute-start(bf16[64,4096]{1,0:T(8,128)(2,1)S(1)} %fusion.2), channel_id=1, source_target_pairs={{0,32},{32,64},{64,96},{96,128},{128,160},{160,192},{192,224},{224... | collective-permute-start | bytes 1572872 | tf_op jit(solution)/shard_map/ppermute | solution.py:17
  261.1 6.1 %collective-permute-done.1 = bf16[64,4096]{1,0:T(8,128)(2,1)S(1)} collective-permute-done((bf16[64,4096]{1,0:T(8,128)(2,1)S(1)}, bf16[64,4096]{1,0:T(8,128)(2,1)S(1)}, u32[]{:S(2)}, u32[]{:S(2)}) %collective-permute-start.1) | collective-permute-done | bytes 524320 | tf_op jit(solution)/shard_map/ppermute | solution.py:17
  267.2 0.8 copy.21
  (11 shorter events, 0.1 us)
Async XLA Ops:
  0.0 64.3 %copy-start = (bf16[1,128,4096]{2,1,0:T(8,128)(2,1)S(1)}, bf16[1,128,4096]{2,1,0:T(8,128)(2,1)}, u32[]{:S(2)}) copy-start(bf16[1,128,4096]{2,1,0:T(8,128)(2,1)} %param.13) | copy-start | bytes 3145732
  4.7 58.9 %copy-start.1 = (bf16[1,4096,128]{2,1,0:T(8,128)(2,1)S(1)}, bf16[1,4096,128]{2,1,0:T(8,128)(2,1)}, u32[]{:S(2)}) copy-start(bf16[1,4096,128]{2,1,0:T(8,128)(2,1)} %param.11) | copy-start | bytes 3145732
  69.3 5.8 %copy-start.6 = (f32[2,1,64,8]{2,3,1,0:T(8,128)S(1)}, f32[2,1,64,8]{2,3,1,0:T(8,128)}, u32[]{:S(2)}) copy-start(f32[2,1,64,8]{2,3,1,0:T(8,128)} %param.9) | copy-start | bytes 12292
  69.3 53.6 %all-to-all-start.1 = ((bf16[32,8,4096]{2,1,0:T(8,128)(2,1)}), bf16[32,8,4096]{2,1,0:T(8,128)(2,1)S(1)}, u32[]{:S(2)}, u32[]{:S(2)}) async-start(bf16[32,8,4096]{2,1,0:T(8,128)(2,1)} %convolution_convert_fusion.1), calls=%async_computation.1 | async-start | bytes 4194304 | tf_op jit(solution)/shard_map/all_to_all | solution.py:58
  122.9 1.0 copy-start.3
  125.0 11.7 %collective-permute-start = (bf16[64,4096]{1,0:T(8,128)(2,1)S(1)}, bf16[64,4096]{1,0:T(8,128)(2,1)S(1)}, u32[]{:S(2)}, u32[]{:S(2)}) collective-permute-start(bf16[64,4096]{1,0:T(8,128)(2,1)S(1)} %fusion.3), channel_id=1, source_target_pairs={{0,32},{32,64},{64,96},{96,128},{128,160},{160,192},{192,224},{224... | collective-permute-start | bytes 1572872 | tf_op jit(solution)/shard_map/ppermute | solution.py:17
  136.7 0.8 copy-start.4
  137.5 55.0 %copy-start.2 = (bf16[1,4096,128]{2,1,0:T(8,128)(2,1)S(1)}, bf16[1,4096,128]{2,1,0:T(8,128)(2,1)}, u32[]{:S(2)}) copy-start(bf16[1,4096,128]{2,1,0:T(8,128)(2,1)} %param.11) | copy-start | bytes 3145732
  198.1 53.3 %all-to-all-start.3 = ((bf16[32,8,4096]{2,1,0:T(8,128)(2,1)}), bf16[32,8,4096]{2,1,0:T(8,128)(2,1)S(1)}, u32[]{:S(2)}, u32[]{:S(2)}) async-start(bf16[32,8,4096]{2,1,0:T(8,128)(2,1)} %convolution_convert_fusion), calls=%async_computation.3 | async-start | bytes 4194304 | tf_op jit(solution)/shard_map/all_to_all | solution.py:58
  251.4 1.0 copy-start.5
  253.5 13.8 %collective-permute-start.1 = (bf16[64,4096]{1,0:T(8,128)(2,1)S(1)}, bf16[64,4096]{1,0:T(8,128)(2,1)S(1)}, u32[]{:S(2)}, u32[]{:S(2)}) collective-permute-start(bf16[64,4096]{1,0:T(8,128)(2,1)S(1)} %fusion.2), channel_id=1, source_target_pairs={{0,32},{32,64},{64,96},{96,128},{128,160},{160,192},{192,224},{224... | collective-permute-start | bytes 1572872 | tf_op jit(solution)/shard_map/ppermute | solution.py:17
where the time goes:
time: 269 us; the launch traced here: 268 us
  blocking collectives  114 us (42%)
  waiting for transfers between devices  108 us (40%)
  starting transfers between devices  24.3 us (9%)
  matrix products  15.1 us (6%)
  local copies, waits for them, and re-layouts  3.81 us (1%)
  other arithmetic  3.2 us (1%)
    all_to_all x2, blocking collectives, moe_layer(): lax.all_to_all(copies, 'expert', split_axis=0, concat_axis=0, tiled=True)  114 us
    all_to_all x2, waiting for transfers between devices, moe_layer(): lax.all_to_all(partial_value, 'expert', split_axis=0, concat_axis=0, tile...  95.7 us
    ppermute x2, starting transfers between devices, passed_along(): return lax.ppermute(value, axis, pairs)  13.2 us
    ppermute x2, waiting for transfers between devices, passed_along(): return lax.ppermute(value, axis, pairs)  11.9 us
    all_to_all x2, starting transfers between devices, moe_layer(): lax.all_to_all(partial_value, 'expert', split_axis=0, concat_axis=0, tile...  11.2 us
    dot_general x2, matrix products, expert_rows(): jnp.einsum('snf,fd->snd', active, w_down, preferred_element_type=jnp.floa...  9.87 us
  transfers between devices with their start and end apart: 4, of which 4 were waited for; matrix products, arithmetic and copies ran while one was open for 0% of the time, Pallas kernels for 0%

commit v1 on v0

v1 whole, which is shorter than its diff:
```python
import functools

import jax
import jax.numpy as jnp
from jax import lax
from jax.experimental import pallas as pl
from jax.experimental.pallas import tpu as pltpu
from jax.sharding import PartitionSpec as P

EPS = 1e-06
TICKS = 2
PAIRS = 4
GROUP = 8
XS = 4
CAP = 8
ORDER = (0, 1, 3, 2)
MESH = pl.DeviceIdType.MESH
F32 = jnp.float32
BF16 = jnp.bfloat16


def kernel(
    hid, ids, rw, gain, wg, wu, wd, out,
    xin, ids_v, rw_v, gain_v, wgu, wd2, xcur, xprev, wloc, wprev, place, packed, rbuf, act, outb, ret,
    loc_sem, wd_send, wd_recv, y_send, y_recv, xf_send, xf_recv, xh_send, xh_recv,
    act_send, act_recv, ret_send, ret_recv, nx_send, nx_recv, nw_send, nw_recv,
):
    segments = lax.axis_size("segment")
    rows, width = xcur.shape
    half = width // 2
    cols = width // GROUP
    s = lax.axis_index("segment")
    p = lax.axis_index("expert")
    pr = p // GROUP
    q = p % GROUP
    b = q // XS
    x = q % XS
    nxt = lax.rem(s + 1, segments)
    prv = lax.rem(s + segments - 1, segments)
    right = lax.rem(x + 1, XS)
    left = lax.rem(x + XS - 1, XS)
    mate = 1 - b

    barrier = pltpu.get_barrier_semaphore()

    def greet(seg, exp):
        pl.semaphore_signal(barrier, inc=1, device_id=(seg, exp), device_id_type=MESH)

    for step in range(1, GROUP):
        greet(s, pr * GROUP + lax.rem(q + step, GROUP))
    for step in range(1, PAIRS):
        for row in range(2):
            greet(s, lax.rem(pr + step, PAIRS) * GROUP + row * XS + x)
    for owner in range(PAIRS * GROUP):
        greet(prv, owner)
    count = GROUP - 1 + 2 * (PAIRS - 1) + PAIRS * GROUP

    loads = [
        (hid.at[0], xin),
        (ids.at[:, 0], ids_v),
        (rw.at[:, 0], rw_v),
        (gain, gain_v),
        (wg.at[0], wgu.at[:, 0:128]),
        (wu.at[0], wgu.at[:, 128:256]),
        (wd.at[0, :, pl.ds(pl.multiple_of(q * cols, 128), cols)], wd2.at[q]),
    ]
    copies = [pltpu.make_async_copy(a, c, loc_sem.at[i]) for i, (a, c) in enumerate(loads)]
    for c in copies:
        c.start()

    def remote(src, dst, send, recv, seg, exp):
        return pltpu.make_async_remote_copy(
            src_ref=src, dst_ref=dst, send_sem=send, recv_sem=recv, device_id=(seg, exp), device_id_type=MESH
        )

    copies[1].wait()
    copies[2].wait()
    lane = lax.broadcasted_iota(jnp.int32, (rows, 128), 1)
    lane_e = lax.rem(lane, 32) // CAP
    lane_c = lax.rem(lane, CAP)
    tri = (
        lax.broadcasted_iota(jnp.int32, (rows, rows), 0) >= lax.broadcasted_iota(jnp.int32, (rows, rows), 1)
    ).astype(F32).astype(BF16)
    for t in range(TICKS):
        share = jnp.zeros((rows, 128), F32)
        member = jnp.zeros((rows, 128), F32)
        idt = ids_v[t]
        rwt = rw_v[t]
        for k in range(idt.shape[1]):
            hit = idt[:, k : k + 1] == lane_e
            share = share + jnp.where(hit, rwt[:, k : k + 1], F32(0.0))
            member = jnp.where(hit, F32(1.0), member)
        rank = jnp.dot(tri, member.astype(BF16), preferred_element_type=F32)
        placed = jnp.where(rank == (lane_c + 1).astype(F32), member, F32(0.0))
        place[t] = placed.astype(BF16)
        weight = placed * share
        high = weight.astype(BF16)
        low = (weight - high.astype(F32)).astype(BF16)
        zero = jnp.zeros_like(weight)
        wloc[t] = jnp.where(lane < 32, high.astype(F32), jnp.where(lane < 64, low.astype(F32), zero)).astype(BF16)

    copies[0].wait()
    copies[3].wait()

    def norm_pack(t, source):
        total = jnp.zeros((rows, 1), F32)
        for j in range(GROUP):
            v = source[:, j * cols : (j + 1) * cols].astype(F32)
            total = total + jnp.sum(v * v, axis=-1, keepdims=True)
        scale = lax.rsqrt(total / width + EPS)
        pick = place[t][:, 0:32]
        for j in range(GROUP):
            v = source[:, j * cols : (j + 1) * cols].astype(F32)
            g = gain_v[0:1, j * cols : (j + 1) * cols].astype(F32)
            normed = (v * scale * g).astype(BF16)
            rowset = lax.dot_general(pick, normed, (((0,), (0,)), ((), ())), preferred_element_type=F32)
            packed[t, :, :, j * cols : (j + 1) * cols] = rowset.astype(BF16).reshape(PAIRS, CAP, cols)

    norm_pack(0, xin)
    pl.semaphore_wait(barrier, count)

    def combine(t, target):
        remote(xprev.at[t], xprev.at[t], nx_send.at[t], nx_recv.at[t], nxt, p).wait_recv()
        remote(wprev.at[t], wprev.at[t], nw_send.at[t], nw_recv.at[t], nxt, p).wait_recv()
        remote(ret.at[t], ret.at[t], ret_send.at[t], ret_recv.at[t], nxt, p).wait_recv()
        w = wprev[t][:, 0:64]
        for j in range(GROUP):
            r = ret[t, :, j].reshape(PAIRS * CAP, cols)
            rr = jnp.concatenate([r, r], axis=0)
            branch = jnp.dot(w, rr, preferred_element_type=F32)
            target(j, xprev[t, :, j * cols : (j + 1) * cols].astype(F32) + branch)

    for t in range(TICKS):
        if t > 0:
            def keep(j, v):
                xcur[:, j * cols : (j + 1) * cols] = v.astype(BF16)

            combine(t - 1, keep)
            norm_pack(t, xcur)
        for d in range(PAIRS):
            dest = lax.rem(pr + PAIRS - ORDER[d], PAIRS)
            targets = [mate] if d == 0 else ([0, 1] if d != 1 else [1, 0])
            for row in targets:
                remote(
                    packed.at[t, dest], rbuf.at[t, pr, q], y_send.at[t], y_recv.at[t * 8 + d * 2 + b],
                    s, dest * GROUP + row * XS + x,
                ).start()
        rbuf[t, pr, q] = packed[t, pr]
        remote(hid.at[0] if t == 0 else xcur, xprev.at[t], nx_send.at[t], nx_recv.at[t], nxt, p).start()
        remote(wloc.at[t], wprev.at[t], nw_send.at[t], nw_recv.at[t], nxt, p).start()

        def block_of(k):
            d, i = k // 2, k % 2
            pp = lax.rem(pr + ORDER[d], PAIRS)
            if d == 0:
                row = b if i == 0 else mate
            elif d == 1:
                row = i
            else:
                row = 1 - i
            return d, pp, row

        def relay(k):
            d, pp, row = block_of(k)
            from_left = rbuf.at[t, pp, row * XS + left]
            from_right = rbuf.at[t, pp, row * XS + right]
            base = pr * GROUP + b * XS
            remote(from_left, from_left, xf_send.at[t], xf_recv.at[t, k, 0], s, base + right).wait_recv()
            part = from_left.at[:, 0:half]
            remote(part, part, xh_send.at[t], xh_recv.at[t, k, 0], s, base + right).start()
            remote(from_right, from_right, xf_send.at[t], xf_recv.at[t, k, 1], s, base + left).wait_recv()
            part = from_right.at[:, half:width]
            remote(part, part, xh_send.at[t], xh_recv.at[t, k, 1], s, base + left).start()

        def gate_up(d):
            base = pr * GROUP + b * XS
            for k in (2 * d, 2 * d + 1):
                _, pp, row = block_of(k)
                far = rbuf.at[t, pp, row * XS + lax.rem(x + 2, XS)]
                for side, span in ((0, (0, half)), (1, (half, width))):
                    part = far.at[:, span[0] : span[1]]
                    remote(part, part, xh_send.at[t], xh_recv.at[t, k, side], s, base + right).wait_recv()
            pp = lax.rem(pr + ORDER[d], PAIRS)
            taken = rbuf[t, pp].reshape(GROUP * CAP, width)
            both = jnp.dot(taken, wgu[...], preferred_element_type=F32)
            gate, up = both[:, 0:128], both[:, 128:256]
            act[t, q, pp] = (gate / (1.0 + jnp.exp(-gate)) * up).astype(BF16)
            for step in range(1, GROUP):
                other = lax.rem(q + step, GROUP)
                remote(
                    act.at[t, q, pp], act.at[t, q, pp], act_send.at[t], act_recv.at[t, d], s, pr * GROUP + other
                ).start()

        for k in range(2 * PAIRS):
            d, pp, row = block_of(k)
            mine = rbuf.at[t, pp, row * XS + x]
            base = pr * GROUP + b * XS
            if k > 0:
                remote(mine, mine, y_send.at[t], y_recv.at[t * 8 + d * 2 + row], s, base + right).wait_recv()
            remote(mine, mine, xf_send.at[t], xf_recv.at[t, k, 0], s, base + right).start()
            remote(mine, mine, xf_send.at[t], xf_recv.at[t, k, 1], s, base + left).start()
            if t == 0 and k > 0:
                other = lax.rem(q + k, GROUP)
                remote(
                    wd.at[0, :, pl.ds(pl.multiple_of(other * cols, 128), cols)], wd2.at[q],
                    wd_send.at[0], wd_recv.at[0], s, pr * GROUP + other,
                ).start()
            if k > 0:
                relay(k - 1)
            if t == 0 and k == 3:
                copies[4].wait()
                copies[5].wait()
            if k % 2 == 1 and k > 1:
                gate_up((k - 3) // 2)
        relay(2 * PAIRS - 1)
        gate_up(PAIRS - 1)

        if t == 0:
            copies[6].wait()
            remote(wd2.at[0:7], wd2.at[0:7], wd_send.at[0], wd_recv.at[0], s, pr * GROUP).wait_recv()
        for d in range(PAIRS):
            remote(act.at[t, 0:7, 0], act.at[t, 0:7, 0], act_send.at[t], act_recv.at[t, d], s, pr * GROUP).wait_recv()
        units = jnp.concatenate([act[t, k].reshape(PAIRS * GROUP * CAP, 128) for k in range(GROUP)], axis=1)
        full = jnp.dot(units, wd2[...].reshape(GROUP * 128, cols), preferred_element_type=F32)
        outb[t] = full.astype(BF16).reshape(PAIRS * GROUP, CAP, cols)
        for step in range(PAIRS * GROUP):
            owner = lax.rem(p + step, PAIRS * GROUP)
            remote(outb.at[t, owner], ret.at[t, pr, q], ret_send.at[t], ret_recv.at[t], nxt, owner).start()

    def emit(j, v):
        out[0, :, j * cols : (j + 1) * cols] = v.astype(BF16)

    combine(TICKS - 1, emit)

    for t in range(TICKS):
        remote(rbuf.at[t, 0, 0:7], rbuf.at[t, 0, 0:7], y_send.at[t], y_recv.at[0], s, p).wait_send()
        remote(rbuf.at[t, 0:2], rbuf.at[t, 0:2], xf_send.at[t], xf_recv.at[t, 0, 0], s, p).wait_send()
        remote(rbuf.at[t, 0], rbuf.at[t, 0], xh_send.at[t], xh_recv.at[t, 0, 0], s, p).wait_send()
        remote(act.at[t, 0:7], act.at[t, 0:7], act_send.at[t], act_recv.at[t, 0], s, p).wait_send()
        remote(ret.at[t], ret.at[t], ret_send.at[t], ret_recv.at[t], s, p).wait_send()
        remote(xprev.at[t], xprev.at[t], nx_send.at[t], nx_recv.at[t], s, p).wait_send()
        remote(wprev.at[t], wprev.at[t], nw_send.at[t], nw_recv.at[t], s, p).wait_send()
    remote(wd2.at[0:7], wd2.at[0:7], wd_send.at[0], wd_recv.at[0], s, p).wait_send()


def body(hidden, expert_ids, route_weights, norm_gain, w_gate, w_up, w_down):
    _, rows, width = hidden.shape
    cols = width // GROUP
    top = expert_ids.shape[-1]
    dma = pltpu.SemaphoreType.DMA
    return pl.pallas_call(
        kernel,
        out_shape=jax.ShapeDtypeStruct(hidden.shape, BF16),
        in_specs=[pl.BlockSpec(memory_space=pl.ANY)] * 7,
        out_specs=pl.BlockSpec(memory_space=pltpu.VMEM),
        scratch_shapes=[
            pltpu.VMEM((rows, width), BF16),
            pltpu.VMEM((TICKS, rows, top), jnp.int32),
            pltpu.VMEM((TICKS, rows, top), F32),
            pltpu.VMEM((1, width), BF16),
            pltpu.VMEM((width, 256), BF16),
            pltpu.VMEM((GROUP, 128, cols), BF16),
            pltpu.VMEM((rows, width), BF16),
            pltpu.VMEM((TICKS, rows, width), BF16),
            pltpu.VMEM((TICKS, rows, 128), BF16),
            pltpu.VMEM((TICKS, rows, 128), BF16),
            pltpu.VMEM((TICKS, rows, 128), BF16),
            pltpu.VMEM((TICKS, PAIRS, CAP, width), BF16),
            pltpu.VMEM((TICKS, PAIRS, GROUP, CAP, width), BF16),
            pltpu.VMEM((TICKS, GROUP, PAIRS, GROUP * CAP, 128), BF16),
            pltpu.VMEM((TICKS, PAIRS * GROUP, CAP, cols), BF16),
            pltpu.VMEM((TICKS, PAIRS, GROUP, CAP, cols), BF16),
            dma((7,)),
            dma((1,)), dma((1,)),
            dma((TICKS,)), dma((TICKS * 8,)),
            dma((TICKS,)), dma((TICKS, 8, 2)),
            dma((TICKS,)), dma((TICKS, 8, 2)),
            dma((TICKS,)), dma((TICKS, PAIRS)),
            dma((TICKS,)), dma((TICKS,)),
            dma((TICKS,)), dma((TICKS,)),
            dma((TICKS,)), dma((TICKS,)),
        ],
        compiler_params=pltpu.CompilerParams(collective_id=0, has_side_effects=True),
    )(hidden, expert_ids, route_weights, norm_gain, w_gate, w_up, w_down)


def solution(mesh):
    return jax.shard_map(
        body,
        mesh=mesh,
        in_specs=(
            P("segment", "expert", None),
            P(None, "segment", "expert", None),
            P(None, "segment", "expert", None),
            P("segment", None),
            P("segment", None, "expert"),
            P("segment", None, "expert"),
            P("segment", "expert", None),
        ),
        out_specs=P("segment", "expert", None),
        check_vma=False,
    )
```

time: 269 us -> 124 us (0.46)
  the two profiles are of different devices: /device:TPU:145 before, /device:TPU:6 now
where the time goes in v1:
time: 124 us; the launch traced here: 122 us
  Pallas kernels  118 us (95%)
  local copies, waits for them, and re-layouts  4.05 us (3%)
    pallas_call x1, Pallas kernels, body(): pl.pallas_call(kernel, out_shape=jax.ShapeDtypeStruct(hidden.shape, BF16)...  118 us
    unnamed x5, local copies, waits for them, and re-layouts  4.05 us

profile of v1, /device:TPU:6, one launch (start us, length us, event | category | flops | bytes accessed | tf_op | source)
XLA Modules:
  0.0 122.0 jit_solution(5337087053460452862)
XLA Ops:
  0.0 0.0 copy-start
  0.0 1.4 %copy.8.ids = s32[2,1,64,8]{3,2,1,0:T(8,128)} copy(s32[2,1,64,8]{2,3,1,0:T(8,128)} %param.8) | data formatting | bytes 8192 | tf_op args[1]
  1.4 0.0 copy-done
  1.4 0.7 copy.9.rw
  2.2 118.0 %shard_map.73 = bf16[1,64,4096]{2,1,0:T(8,128)(2,1)} custom-call(bf16[1,64,4096]{2,1,0:T(8,128)(2,1)} %hid.1, s32[2,1,64,8]{3,2,1,0:T(8,128)} %copy.8.ids, f32[2,1,64,8]{3,2,1,0:T(8,128)} %copy.9.rw, bf16[1,4096]{1,0:T(2,128)(2,1)} %gain.1, bf16[1,4096,128]{2,1,0:T(8,128)(2,1)} %wg.1, bf16[1,4096,128]{2,1,0:T(8,128)(2,1)} %wu.1, bf16[1,128,4096]{2,1,0:T(8,128)(2,1)} %wd.1), custom_call_target="tpu_custom_call" | custom-call | tf_op jit(solution)/shard_map/pallas_call | solution.py:251
  120.2 1.9 %copy.11 = bf16[1,64,4096]{2,1,0:T(8,128)(2,1)} copy(bf16[1,64,4096]{2,1,0:T(8,128)(2,1)} %shard_map.73) | data formatting | bytes 1048576
Async XLA Ops:
  0.0 1.4 %copy-start = (f32[2,1,64,8]{2,3,1,0:T(8,128)S(1)}, f32[2,1,64,8]{2,3,1,0:T(8,128)}, u32[]{:S(2)}) copy-start(f32[2,1,64,8]{2,3,1,0:T(8,128)} %param.9) | copy-start | bytes 12292

commit v2 on v1

v2 whole, which is shorter than its diff:
```python
import functools

import jax
import jax.numpy as jnp
from jax import lax
from jax.experimental import pallas as pl
from jax.experimental.pallas import tpu as pltpu
from jax.sharding import PartitionSpec as P

EPS = 1e-06
TICKS = 2
PAIRS = 4
GROUP = 8
XS = 4
CAP = 8
MESH = pl.DeviceIdType.MESH
F32 = jnp.float32
BF16 = jnp.bfloat16

def combined(x, w, r):
    r = r.reshape(PAIRS * CAP, r.shape[-1])
    branch = jnp.dot(w[:, 0:64], jnp.concatenate([r, r], axis=0), preferred_element_type=F32)
    return (x.astype(F32) + branch).astype(BF16)


def finish(x_ref, w_ref, r_ref, o_ref):
    step = 512
    for j in range(x_ref.shape[1] // step):
        span = slice(j * step, (j + 1) * step)
        o_ref[0, :, span] = combined(x_ref[:, span], w_ref[...], r_ref[:, :, span])


NEAR = (0, 1, -1, -2, 2, -3, 3, 4)
CHUNKS = ((0, 1), (2, 3), (4, 6), (5, 7))
STEPS_OUT = ((1, 1), (-1, -1), (2, -2), (-3, -3))
PLAN = (
    ("S0", "W+1", "W-1", "S1", "S2", "Wm", "R0", "S3", "R1", "S4", "W+5", "W-5", "R2", "S5", "R3", "G0", "S6", "R4", "W2", "S7", "R5", "G1", "R6", "R7", "W6", "G2", "G3", "V", "D0", "D1", "D2", "D3"),
    ("S0", "S1", "S2", "R0", "S3", "R1", "S4", "R2", "S5", "R3", "G0", "S6", "R4", "S7", "R5", "G1", "R6", "R7", "G2", "D0", "G3", "D1", "D2", "D3"),
)


def kernel(
    hid, ids, rw, gain, wg, wu, wd, x_out, w_out, r_out,
    xin, ids_v, rw_v, gain_v, wgu, wd2, xcur, xprev, wloc, wprev, place, packed, rbuf, act, outb, ret,
    loc_sem, wd_send, wd_recv, y_send, y_recv, xf_send, xf_recv, xh_send, xh_recv,
    act_send, act_recv, ret_send, ret_recv, nx_send, nx_recv, nw_send, nw_recv,
):
    segments = lax.axis_size("segment")
    rows, width = xcur.shape
    half = width // 2
    cols = width // GROUP
    s = lax.axis_index("segment")
    p = lax.axis_index("expert")
    pr = p // GROUP
    q = p % GROUP
    b = q // XS
    x = q % XS
    y = p // XS
    nxt = lax.rem(s + 1, segments)
    prv = lax.rem(s + segments - 1, segments)
    right = lax.rem(x + 1, XS)
    left = lax.rem(x + XS - 1, XS)
    across = lax.rem(x + 2, XS)
    home = y * XS
    sign = 1 - 2 * b

    def row_of(offset):
        return lax.rem(y + sign * offset + 16, 8)

    loads = [
        (ids.at[:, 0], ids_v),
        (rw.at[:, 0], rw_v),
        (hid.at[0], xin),
        (gain, gain_v),
        (wg.at[0], wgu.at[:, 0:128]),
        (wu.at[0], wgu.at[:, 128:256]),
        (wd.at[0, :, pl.ds(pl.multiple_of(q * cols, 128), cols)], wd2.at[q]),
    ]
    copies = [pltpu.make_async_copy(a, c, loc_sem.at[i]) for i, (a, c) in enumerate(loads)]
    for c in copies[:4]:
        c.start()

    barrier = pltpu.get_barrier_semaphore()

    def greet(seg, exp):
        pl.semaphore_signal(barrier, inc=1, device_id=(seg, exp), device_id_type=MESH)

    greet(prv, p)
    for step in range(1, GROUP):
        greet(s, pr * GROUP + lax.rem(q + step, GROUP))
    for offset in (-1, -2, -3):
        greet(s, row_of(offset) * XS + x)
    count = 1 + GROUP - 1 + 3
    for c in copies[4:]:
        c.start()

    def remote(src, dst, send, recv, seg, exp):
        return pltpu.make_async_remote_copy(
            src_ref=src, dst_ref=dst, send_sem=send, recv_sem=recv, device_id=(seg, exp), device_id_type=MESH
        )

    copies[0].wait()
    copies[1].wait()
    lane = lax.broadcasted_iota(jnp.int32, (rows, 128), 1)
    lane_e = lax.rem(lane, 32) // CAP
    lane_c = lax.rem(lane, CAP)
    tri = (
        lax.broadcasted_iota(jnp.int32, (rows, rows), 0) >= lax.broadcasted_iota(jnp.int32, (rows, rows), 1)
    ).astype(F32).astype(BF16)
    for t in range(TICKS):
        share = jnp.zeros((rows, 128), F32)
        member = jnp.zeros((rows, 128), F32)
        idt = jnp.transpose(ids_v[t])
        rwt = jnp.transpose(rw_v[t])
        for k in range(idt.shape[1]):
            hit = idt[:, k : k + 1] == lane_e
            share = share + jnp.where(hit, rwt[:, k : k + 1], F32(0.0))
            member = jnp.where(hit, F32(1.0), member)
        rank = jnp.dot(tri, member.astype(BF16), preferred_element_type=F32)
        placed = jnp.where(rank == (lane_c + 1).astype(F32), member, F32(0.0))
        place[t] = placed.astype(BF16)
        weight = placed * share
        high = weight.astype(BF16)
        low = (weight - high.astype(F32)).astype(BF16)
        zero = jnp.zeros_like(weight)
        wloc[t] = jnp.where(lane < 32, high.astype(F32), jnp.where(lane < 64, low.astype(F32), zero)).astype(BF16)

    def norm_pack(t, source):
        total = jnp.zeros((rows, 1), F32)
        for j in range(GROUP):
            v = source[:, j * cols : (j + 1) * cols].astype(F32)
            total = total + jnp.sum(v * v, axis=-1, keepdims=True)
        scale = lax.rsqrt(total / width + EPS)
        pick = place[t][:, 0:32]
        for j in range(GROUP):
            v = source[:, j * cols : (j + 1) * cols].astype(F32)
            g = gain_v[0:1, j * cols : (j + 1) * cols].astype(F32)
            normed = (v * scale * g).astype(BF16)
            rowset = lax.dot_general(pick, normed, (((0,), (0,)), ((), ())), preferred_element_type=F32)
            packed[t, :, :, j * cols : (j + 1) * cols] = rowset.astype(BF16).reshape(PAIRS, CAP, cols)

    copies[2].wait()
    copies[3].wait()
    norm_pack(0, xin)
    pl.semaphore_wait(barrier, count)

    def landing(t):
        return (xprev, wprev, ret) if t < TICKS - 1 else (x_out, w_out, r_out)

    def arrive(t):
        at, wt, rt = landing(t)
        remote(at, at, nx_send.at[t], nx_recv.at[t], nxt, p).wait_recv()
        remote(wt, wt, nw_send.at[t], nw_recv.at[t], nxt, p).wait_recv()
        remote(rt, rt, ret_send.at[t], ret_recv.at[t], nxt, p).wait_recv()

    def pair_of(c):
        return row_of(NEAR[CHUNKS[c][0]]) // 2

    def kind_of(c):
        return (0, 2 - b, 1 + b, 3)[c]

    for t in range(TICKS):
        if t > 0:
            arrive(t - 1)
            for j in range(GROUP):
                span = slice(j * cols, (j + 1) * cols)
                xcur[:, span] = combined(xprev[:, span], wprev[...], ret[:, :, span])
            norm_pack(t, xcur)

        def cell(k, column):
            row = row_of(NEAR[k])
            return rbuf.at[t, row // 2, lax.rem(row, 2) * XS + column]

        def send(k):
            mine = cell(k, x)
            if k > 0:
                remote(mine, mine, y_send.at[t], y_recv.at[t * 8 + k], s, home + right).wait_recv()
            remote(mine, mine, xf_send.at[t], xf_recv.at[t, k, 0], s, home + right).start()
            remote(mine, mine, xf_send.at[t], xf_recv.at[t, k, 1], s, home + left).start()
            if NEAR[k] < 0:
                onward = NEAR.index(1 - NEAR[k])
                remote(mine, mine, y_send.at[t], y_recv.at[t * 8 + onward], s, row_of(1) * XS + x).start()

        def relay(k):
            from_left, from_right = cell(k, left), cell(k, right)
            remote(from_left, from_left, xf_send.at[t], xf_recv.at[t, k, 0], s, home + right).wait_recv()
            part = from_left.at[:, 0:half]
            remote(part, part, xh_send.at[t], xh_recv.at[t, k, 0], s, home + right).start()
            remote(from_right, from_right, xf_send.at[t], xf_recv.at[t, k, 1], s, home + left).wait_recv()
            part = from_right.at[:, half:width]
            remote(part, part, xh_send.at[t], xh_recv.at[t, k, 1], s, home + left).start()

        def gate_up(c):
            if t == 0 and c == 0:
                copies[4].wait()
                copies[5].wait()
            for k in CHUNKS[c]:
                far = cell(k, across)
                for side, span in ((0, (0, half)), (1, (half, width))):
                    part = far.at[:, span[0] : span[1]]
                    remote(part, part, xh_send.at[t], xh_recv.at[t, k, side], s, home + right).wait_recv()
            pp = pair_of(c)
            taken = rbuf[t, pp].reshape(GROUP * CAP, width)
            both = jnp.dot(taken, wgu[...], preferred_element_type=F32)
            gate, up = both[:, 0:128], both[:, 128:256]
            act[t, q, pp] = (gate / (1.0 + jnp.exp(-gate)) * up).astype(BF16)
            mine = act.at[t, q, pp]
            for step in (1, 3, 5, 7, 4, 2, 6):
                other = lax.rem(q + step, GROUP)
                remote(
                    mine, mine, act_send.at[t], act_recv.at[t * PAIRS + kind_of(c)], s, pr * GROUP + other
                ).start()

        def resplit(other):
            remote(
                wd.at[0, :, pl.ds(pl.multiple_of(other * cols, 128), cols)], wd2.at[q],
                wd_send.at[0], wd_recv.at[0], s, pr * GROUP + other,
            ).start()

        def down(c):
            pp = lax.rem(pr + (0, 1, 3, 2)[c], PAIRS)
            kind = (0, 1, 2, 3)[c]
            block = act.at[t, 0:7, 0]
            remote(block, block, act_send.at[t], act_recv.at[t * PAIRS + kind], s, pr * GROUP).wait_recv()
            units = jnp.concatenate([act[t, k, pp] for k in range(GROUP)], axis=1)
            full = jnp.dot(units, wd2[...].reshape(GROUP * 128, cols), preferred_element_type=F32)
            outb[t, pp] = full.astype(BF16).reshape(GROUP, CAP, cols)
            for step in range(GROUP):
                owner = lax.rem(q + step, GROUP)
                remote(
                    outb.at[t, pp, owner], there_r.at[pr, :, pl.ds(pl.multiple_of(q * cols, 128), cols)],
                    ret_send.at[t], ret_recv.at[t], nxt, pp * GROUP + owner,
                ).start()

        for offset, seen in STEPS_OUT:
            target = row_of(offset)
            remote(
                packed.at[t, target // 2], rbuf.at[t, pr, q], y_send.at[t], y_recv.at[t * 8 + NEAR.index(seen)],
                s, target * XS + x,
            ).start()
        rbuf[t, pr, q] = packed[t, pr]
        there_x, there_w, there_r = landing(t)
        remote(hid.at[0] if t == 0 else xcur, there_x, nx_send.at[t], nx_recv.at[t], nxt, p).start()
        remote(wloc.at[t], there_w, nw_send.at[t], nw_recv.at[t], nxt, p).start()

        for step in PLAN[t]:
            what, arg = step[0], step[1:]
            if what == "S":
                send(int(arg))
            elif what == "R":
                relay(int(arg))
            elif what == "G":
                gate_up(int(arg))
            elif what == "D":
                down(int(arg))
            elif what == "V":
                copies[6].wait()
                remote(wd2.at[0:7], wd2.at[0:7], wd_send.at[0], wd_recv.at[0], s, pr * GROUP).wait_recv()
            else:
                column = {"+1": right, "-1": left, "2": across, "m": x, "+5": right, "-5": left, "6": across}[arg]
                resplit((b if arg in ("+1", "-1", "2") else 1 - b) * XS + column)

    arrive(TICKS - 1)
    for t in range(TICKS):
        remote(rbuf.at[t, 0, 0:7], rbuf.at[t, 0, 0:7], y_send.at[t], y_recv.at[0], s, p).wait_send()
        remote(rbuf.at[t, 0:2], rbuf.at[t, 0:2], xf_send.at[t], xf_recv.at[t, 0, 0], s, p).wait_send()
        remote(rbuf.at[t, 0], rbuf.at[t, 0], xh_send.at[t], xh_recv.at[t, 0, 0], s, p).wait_send()
        remote(act.at[t, 0:7], act.at[t, 0:7], act_send.at[t], act_recv.at[0], s, p).wait_send()
        remote(ret, ret, ret_send.at[t], ret_recv.at[t], s, p).wait_send()
        remote(xprev, xprev, nx_send.at[t], nx_recv.at[t], s, p).wait_send()
        remote(wprev, wprev, nw_send.at[t], nw_recv.at[t], s, p).wait_send()
    remote(wd2.at[0:7], wd2.at[0:7], wd_send.at[0], wd_recv.at[0], s, p).wait_send()


def body(hidden, expert_ids, route_weights, norm_gain, w_gate, w_up, w_down):
    _, rows, width = hidden.shape
    cols = width // GROUP
    top = expert_ids.shape[-1]
    dma = pltpu.SemaphoreType.DMA
    landed = pl.pallas_call(
        kernel,
        out_shape=(
            jax.ShapeDtypeStruct((rows, width), BF16),
            jax.ShapeDtypeStruct((rows, 128), BF16),
            jax.ShapeDtypeStruct((PAIRS, CAP, width), BF16),
        ),
        in_specs=[pl.BlockSpec(memory_space=pl.ANY)] * 7,
        out_specs=[pl.BlockSpec(memory_space=pl.ANY)] * 3,
        scratch_shapes=[
            pltpu.VMEM((rows, width), BF16),
            pltpu.VMEM((TICKS, top, rows), jnp.int32),
            pltpu.VMEM((TICKS, top, rows), F32),
            pltpu.VMEM((1, width), BF16),
            pltpu.VMEM((width, 256), BF16),
            pltpu.VMEM((GROUP, 128, cols), BF16),
            pltpu.VMEM((rows, width), BF16),
            pltpu.VMEM((rows, width), BF16),
            pltpu.VMEM((TICKS, rows, 128), BF16),
            pltpu.VMEM((rows, 128), BF16),
            pltpu.VMEM((TICKS, rows, 128), BF16),
            pltpu.VMEM((TICKS, PAIRS, CAP, width), BF16),
            pltpu.VMEM((TICKS, PAIRS, GROUP, CAP, width), BF16),
            pltpu.VMEM((TICKS, GROUP, PAIRS, GROUP * CAP, 128), BF16),
            pltpu.VMEM((TICKS, PAIRS, GROUP, CAP, cols), BF16),
            pltpu.VMEM((PAIRS, CAP, width), BF16),
            dma((7,)),
            dma((1,)), dma((1,)),
            dma((TICKS,)), dma((TICKS * 8,)),
            dma((TICKS,)), dma((TICKS, 8, 2)),
            dma((TICKS,)), dma((TICKS, 8, 2)),
            dma((TICKS,)), dma((TICKS * PAIRS,)),
            dma((TICKS,)), dma((TICKS,)),
            dma((TICKS,)), dma((TICKS,)),
            dma((TICKS,)), dma((TICKS,)),
        ],
        compiler_params=pltpu.CompilerParams(collective_id=0, has_side_effects=True),
    )(hidden, jnp.swapaxes(expert_ids, 2, 3), jnp.swapaxes(route_weights, 2, 3), norm_gain, w_gate, w_up, w_down)
    part = width // 2
    return pl.pallas_call(
        finish,
        grid=(2,),
        out_shape=jax.ShapeDtypeStruct(hidden.shape, BF16),
        in_specs=[
            pl.BlockSpec((rows, part), lambda i: (0, i)),
            pl.BlockSpec((rows, 128), lambda i: (0, 0)),
            pl.BlockSpec((PAIRS, CAP, part), lambda i: (0, 0, i)),
        ],
        out_specs=pl.BlockSpec((1, rows, part), lambda i: (0, 0, i)),
    )(*landed)


def solution(mesh):
    return jax.shard_map(
        body,
        mesh=mesh,
        in_specs=(
            P("segment", "expert", None),
            P(None, "segment", "expert", None),
            P(None, "segment", "expert", None),
            P("segment", None),
            P("segment", None, "expert"),
            P("segment", None, "expert"),
            P("segment", "expert", None),
        ),
        out_specs=P("segment", "expert", None),
        check_vma=False,
    )
```

time: 124 us -> 107 us (0.86)
  Pallas kernels: 118 us -> 106 us
  local copies, waits for them, and re-layouts: 4.05 us -> 0 us
    pallas_call x1 -> x2, Pallas kernels: 118 us -> 106 us  [the longest x1 104 us: body(): pl.pallas_call(kernel, out_shape=(jax.ShapeDtypeStruct((rows, width), BF1...]
    unnamed x5 -> x0, local copies, waits for them, and re-layouts: 4.05 us -> none
where the time goes in v2:
time: 107 us; the launch traced here: 106 us
  Pallas kernels  106 us (99%)
    pallas_call x1, Pallas kernels, body(): pl.pallas_call(kernel, out_shape=(jax.ShapeDtypeStruct((rows, width), BF1...  104 us

profile of v2, /device:TPU:6, one launch (start us, length us, event | category | flops | bytes accessed | tf_op | source)
XLA Modules:
  0.0 105.7 jit_solution(10101625560106829449)
XLA Ops:
  0.0 103.6 %shard_map.73 = (bf16[64,4096]{1,0:T(8,128)(2,1)}, bf16[64,128]{1,0:T(8,128)(2,1)}, bf16[4,8,4096]{2,1,0:T(8,128)(2,1)}) custom-call(bf16[1,64,4096]{2,1,0:T(8,128)(2,1)} %hid.1, s32[2,1,8,64]{3,2,1,0:T(8,128)} %bitcast.2, f32[2,1,8,64]{3,2,1,0:T(8,128)} %bitcast.3, bf16[1,4096]{1,0:T(2,128)(2,1)} %gain.1, bf16[1,4096,128]{2,1,0:T(8,128)(2,1)} %wg.1, ...), custom_call_target="tpu_custom_call" | custom-call | tf_op jit(solution)/shard_map/pallas_call | solution.py:280
  103.6 2.1 %shard_map.74 = bf16[1,64,4096]{2,1,0:T(8,128)(2,1)} custom-call(bf16[64,4096]{1,0:T(8,128)(2,1)} %get-tuple-element.8.x_ref, bf16[64,128]{1,0:T(8,128)(2,1)} %get-tuple-element.9.w_ref, bf16[4,8,4096]{2,1,0:T(8,128)(2,1)} %get-tuple-element.10.r_ref), custom_call_target="tpu_custom_call" | custom-call | tf_op jit(solution)/shard_map/pallas_call | solution.py:319

commit v3 on v2

--- a/solution.py
+++ b/solution.py
@@ -30,12 +30,13 @@
         o_ref[0, :, span] = combined(x_ref[:, span], w_ref[...], r_ref[:, :, span])
 
 
-NEAR = (0, 1, -1, -2, 2, -3, 3, 4)
-CHUNKS = ((0, 1), (2, 3), (4, 6), (5, 7))
+NEAR = (0, -1, -2, -3, 2, 3, 1, 4)
+WHOLE, HANDED = 3, 7
+CHUNKS = ((0, 6), (1, 2), (4, 5), (3, 7))
 STEPS_OUT = ((1, 1), (-1, -1), (2, -2), (-3, -3))
 PLAN = (
-    ("S0", "W+1", "W-1", "S1", "S2", "Wm", "R0", "S3", "R1", "S4", "W+5", "W-5", "R2", "S5", "R3", "G0", "S6", "R4", "W2", "S7", "R5", "G1", "R6", "R7", "W6", "G2", "G3", "V", "D0", "D1", "D2", "D3"),
-    ("S0", "S1", "S2", "R0", "S3", "R1", "S4", "R2", "S5", "R3", "G0", "S6", "R4", "S7", "R5", "G1", "R6", "R7", "G2", "D0", "G3", "D1", "D2", "D3"),
+    ("S0", "W+1", "W-1", "S1", "S2", "Wm", "R0", "S3", "R1", "S4", "W+5", "W-5", "R2", "S5", "R3", "S6", "G1", "R4", "W2", "F", "R5", "G3", "R6", "W6", "G2", "G0", "V", "D3", "D1", "D2", "D0"),
+    ("S0", "S1", "S2", "R0", "S3", "R1", "S4", "R2", "S5", "R3", "S6", "G1", "R4", "F", "R5", "G3", "R6", "G2", "D3", "G0", "D1", "D2", "D0"),
 )
 
 
@@ -171,6 +172,19 @@
             row = row_of(NEAR[k])
             return rbuf.at[t, row // 2, lax.rem(row, 2) * XS + column]
 
+        def hand(block, arrived):
+            remote(block, block, y_send.at[t], arrived, s, row_of(1) * XS + x).start()
+
+        def far_halves(k):
+            far = cell(k, across)
+            for side, span in ((0, (0, half)), (1, (half, width))):
+                part = far.at[:, span[0] : span[1]]
+                remote(part, part, xh_send.at[t], xh_recv.at[t, k, side], s, home + right).wait_recv()
+
+        def hand_far():
+            far_halves(WHOLE)
+            hand(cell(WHOLE, across), xh_recv.at[t, HANDED, 0])
+
         def send(k):
             mine = cell(k, x)
             if k > 0:
@@ -179,7 +193,7 @@
             remote(mine, mine, xf_send.at[t], xf_recv.at[t, k, 1], s, home + left).start()
             if NEAR[k] < 0:
                 onward = NEAR.index(1 - NEAR[k])
-                remote(mine, mine, y_send.at[t], y_recv.at[t * 8 + onward], s, row_of(1) * XS + x).start()
+                hand(mine, y_recv.at[t * 8 + onward])
 
         def relay(k):
             from_left, from_right = cell(k, left), cell(k, right)
@@ -189,16 +203,26 @@
             remote(from_right, from_right, xf_send.at[t], xf_recv.at[t, k, 1], s, home + left).wait_recv()
             part = from_right.at[:, half:width]
             remote(part, part, xh_send.at[t], xh_recv.at[t, k, 1], s, home + left).start()
+            if k == WHOLE:
+                hand(from_left, xf_recv.at[t, HANDED, 0])
+                hand(from_right, xf_recv.at[t, HANDED, 1])
 
         def gate_up(c):
-            if t == 0 and c == 0:
+            if t == 0 and c == 1:
                 copies[4].wait()
                 copies[5].wait()
             for k in CHUNKS[c]:
-                far = cell(k, across)
-                for side, span in ((0, (0, half)), (1, (half, width))):
-                    part = far.at[:, span[0] : span[1]]
-                    remote(part, part, xh_send.at[t], xh_recv.at[t, k, side], s, home + right).wait_recv()
+                if k == HANDED:
+                    for column, arrived in (
+                        (x, y_recv.at[t * 8 + k]),
+                        (left, xf_recv.at[t, k, 0]),
+                        (right, xf_recv.at[t, k, 1]),
+                        (across, xh_recv.at[t, k, 0]),
+                    ):
+                        block = cell(k, column)
+                        remote(block, block, y_send.at[t], arrived, s, row_of(1) * XS + x).wait_recv()
+                elif k != WHOLE:
+                    far_halves(k)
             pp = pair_of(c)
             taken = rbuf[t, pp].reshape(GROUP * CAP, width)
             both = jnp.dot(taken, wgu[...], preferred_element_type=F32)
@@ -249,6 +273,8 @@
                 send(int(arg))
             elif what == "R":
                 relay(int(arg))
+            elif what == "F":
+                hand_far()
             elif what == "G":
                 gate_up(int(arg))
             elif what == "D":
@@ -262,9 +288,9 @@
 
     arrive(TICKS - 1)
     for t in range(TICKS):
-        remote(rbuf.at[t, 0, 0:7], rbuf.at[t, 0, 0:7], y_send.at[t], y_recv.at[0], s, p).wait_send()
-        remote(rbuf.at[t, 0:2], rbuf.at[t, 0:2], xf_send.at[t], xf_recv.at[t, 0, 0], s, p).wait_send()
-        remote(rbuf.at[t, 0], rbuf.at[t, 0], xh_send.at[t], xh_recv.at[t, 0, 0], s, p).wait_send()
+        remote(rbuf.at[t, 0:2, 0:5], rbuf.at[t, 0:2, 0:5], y_send.at[t], y_recv.at[0], s, p).wait_send()
+        remote(rbuf.at[t, 0:2, 0:7], rbuf.at[t, 0:2, 0:7], xf_send.at[t], xf_recv.at[t, 0, 0], s, p).wait_send()
+        remote(rbuf.at[t, 0, 0:7], rbuf.at[t, 0, 0:7], xh_send.at[t], xh_recv.at[t, 0, 0], s, p).wait_send()
         remote(act.at[t, 0:7], act.at[t, 0:7], act_send.at[t], act_recv.at[0], s, p).wait_send()
         remote(ret, ret, ret_send.at[t], ret_recv.at[t], s, p).wait_send()
         remote(xprev, xprev, nx_send.at[t], nx_recv.at[t], s, p).wait_send()

time: 107 us -> 102 us (0.953)
  Pallas kernels: 106 us -> 100 us
    pallas_call x1, Pallas kernels: 104 us -> 98.3 us  [body(): pl.pallas_call(kernel, out_shape=(jax.ShapeDtypeStruct((rows, width), BF1...]
where the time goes in v3:
time: 102 us; the launch traced here: 100 us
  Pallas kernels  100 us (98%)
    pallas_call x1, Pallas kernels, body(): pl.pallas_call(kernel, out_shape=(jax.ShapeDtypeStruct((rows, width), BF1...  98.3 us
    pallas_call x1, Pallas kernels, body(): pl.pallas_call(finish, grid=(2,), out_shape=jax.ShapeDtypeStruct(hidden.s...  2.14 us

profile of v3, /device:TPU:6, one launch (start us, length us, event | category | flops | bytes accessed | tf_op | source)
XLA Modules:
  0.0 100.5 jit_solution(3573356232329915099)
XLA Ops:
  0.0 98.3 %shard_map.73 = (bf16[64,4096]{1,0:T(8,128)(2,1)}, bf16[64,128]{1,0:T(8,128)(2,1)}, bf16[4,8,4096]{2,1,0:T(8,128)(2,1)}) custom-call(bf16[1,64,4096]{2,1,0:T(8,128)(2,1)} %hid.1, s32[2,1,8,64]{3,2,1,0:T(8,128)} %bitcast.2, f32[2,1,8,64]{3,2,1,0:T(8,128)} %bitcast.3, bf16[1,4096]{1,0:T(2,128)(2,1)} %gain.1, bf16[1,4096,128]{2,1,0:T(8,128)(2,1)} %wg.1, ...), custom_call_target="tpu_custom_call" | custom-call | tf_op jit(solution)/shard_map/pallas_call | solution.py:306
  98.3 2.1 %shard_map.74 = bf16[1,64,4096]{2,1,0:T(8,128)(2,1)} custom-call(bf16[64,4096]{1,0:T(8,128)(2,1)} %get-tuple-element.8.x_ref, bf16[64,128]{1,0:T(8,128)(2,1)} %get-tuple-element.9.w_ref, bf16[4,8,4096]{2,1,0:T(8,128)(2,1)} %get-tuple-element.10.r_ref), custom_call_target="tpu_custom_call" | custom-call | tf_op jit(solution)/shard_map/pallas_call | solution.py:345

commit v4 on v3

--- a/solution.py
+++ b/solution.py
@@ -32,11 +32,12 @@
 
 NEAR = (0, -1, -2, -3, 2, 3, 1, 4)
 WHOLE, HANDED = 3, 7
+DIRECT = 6
 CHUNKS = ((0, 6), (1, 2), (4, 5), (3, 7))
 STEPS_OUT = ((1, 1), (-1, -1), (2, -2), (-3, -3))
 PLAN = (
-    ("S0", "W+1", "W-1", "S1", "S2", "Wm", "R0", "S3", "R1", "S4", "W+5", "W-5", "R2", "S5", "R3", "S6", "G1", "R4", "W2", "F", "R5", "G3", "R6", "W6", "G2", "G0", "V", "D3", "D1", "D2", "D0"),
-    ("S0", "S1", "S2", "R0", "S3", "R1", "S4", "R2", "S5", "R3", "S6", "G1", "R4", "F", "R5", "G3", "R6", "G2", "D3", "G0", "D1", "D2", "D0"),
+    ("S0", "W+1", "W-1", "S1", "S2", "Wm", "R0", "S3", "R1", "S4", "W+5", "W-5", "R2", "S5", "R3", "R4", "S6", "G1", "R5", "W2", "F", "W6", "G3", "G2", "G0", "V", "D3", "D1", "D2", "D0"),
+    ("S0", "S1", "S2", "R0", "S3", "R1", "S4", "R2", "S5", "R3", "R4", "S6", "G1", "R5", "F", "G3", "G2", "G0", "D3", "D1", "D2", "D0"),
 )
 
 
@@ -177,6 +178,12 @@
 
         def far_halves(k):
             far = cell(k, across)
+            if k == DIRECT:
+                near_left, near_right = cell(k, left), cell(k, right)
+                remote(near_left, near_left, xf_send.at[t], xf_recv.at[t, k, 0], s, home + right).wait_recv()
+                remote(near_right, near_right, xf_send.at[t], xf_recv.at[t, k, 1], s, home + left).wait_recv()
+                remote(far, far, xf_send.at[t], xh_recv.at[t, k, 0], s, home + right).wait_recv()
+                return
             for side, span in ((0, (0, half)), (1, (half, width))):
                 part = far.at[:, span[0] : span[1]]
                 remote(part, part, xh_send.at[t], xh_recv.at[t, k, side], s, home + right).wait_recv()
@@ -191,6 +198,8 @@
                 remote(mine, mine, y_send.at[t], y_recv.at[t * 8 + k], s, home + right).wait_recv()
             remote(mine, mine, xf_send.at[t], xf_recv.at[t, k, 0], s, home + right).start()
             remote(mine, mine, xf_send.at[t], xf_recv.at[t, k, 1], s, home + left).start()
+            if k == DIRECT:
+                remote(mine, mine, xf_send.at[t], xh_recv.at[t, k, 0], s, home + across).start()
             if NEAR[k] < 0:
                 onward = NEAR.index(1 - NEAR[k])
                 hand(mine, y_recv.at[t * 8 + onward])
@@ -289,8 +298,8 @@
     arrive(TICKS - 1)
     for t in range(TICKS):
         remote(rbuf.at[t, 0:2, 0:5], rbuf.at[t, 0:2, 0:5], y_send.at[t], y_recv.at[0], s, p).wait_send()
-        remote(rbuf.at[t, 0:2, 0:7], rbuf.at[t, 0:2, 0:7], xf_send.at[t], xf_recv.at[t, 0, 0], s, p).wait_send()
-        remote(rbuf.at[t, 0, 0:7], rbuf.at[t, 0, 0:7], xh_send.at[t], xh_recv.at[t, 0, 0], s, p).wait_send()
+        remote(rbuf.at[t, 0:3, 0:5], rbuf.at[t, 0:3, 0:5], xf_send.at[t], xf_recv.at[t, 0, 0], s, p).wait_send()
+        remote(rbuf.at[t, 0, 0:6], rbuf.at[t, 0, 0:6], xh_send.at[t], xh_recv.at[t, 0, 0], s, p).wait_send()
         remote(act.at[t, 0:7], act.at[t, 0:7], act_send.at[t], act_recv.at[0], s, p).wait_send()
         remote(ret, ret, ret_send.at[t], ret_recv.at[t], s, p).wait_send()
         remote(xprev, xprev, nx_send.at[t], nx_recv.at[t], s, p).wait_send()

time: 102 us -> 103 us (level); the launches traced: 100 us -> 103 us
  Pallas kernels: 100 us -> 103 us
    pallas_call x1, Pallas kernels: 98.3 us -> 100 us  [body(): pl.pallas_call(kernel, out_shape=(jax.ShapeDtypeStruct((rows, width), BF1...]
where the time goes in v4:
time: 103 us
  Pallas kernels  103 us (100%)
    pallas_call x1, Pallas kernels, body(): pl.pallas_call(kernel, out_shape=(jax.ShapeDtypeStruct((rows, width), BF1...  100 us
    pallas_call x1, Pallas kernels, body(): pl.pallas_call(finish, grid=(2,), out_shape=jax.ShapeDtypeStruct(hidden.s...  2.15 us

profile of v4, /device:TPU:6, one launch (start us, length us, event | category | flops | bytes accessed | tf_op | source)
XLA Modules:
  0.0 102.6 jit_solution(17745345153190294184)
XLA Ops:
  0.0 100.4 %shard_map.73 = (bf16[64,4096]{1,0:T(8,128)(2,1)}, bf16[64,128]{1,0:T(8,128)(2,1)}, bf16[4,8,4096]{2,1,0:T(8,128)(2,1)}) custom-call(bf16[1,64,4096]{2,1,0:T(8,128)(2,1)} %hid.1, s32[2,1,8,64]{3,2,1,0:T(8,128)} %bitcast.2, f32[2,1,8,64]{3,2,1,0:T(8,128)} %bitcast.3, bf16[1,4096]{1,0:T(2,128)(2,1)} %gain.1, bf16[1,4096,128]{2,1,0:T(8,128)(2,1)} %wg.1, ...), custom_call_target="tpu_custom_call" | custom-call | tf_op jit(solution)/shard_map/pallas_call | solution.py:315
  100.4 2.1 %shard_map.74 = bf16[1,64,4096]{2,1,0:T(8,128)(2,1)} custom-call(bf16[64,4096]{1,0:T(8,128)(2,1)} %get-tuple-element.8.x_ref, bf16[64,128]{1,0:T(8,128)(2,1)} %get-tuple-element.9.w_ref, bf16[4,8,4096]{2,1,0:T(8,128)(2,1)} %get-tuple-element.10.r_ref), custom_call_target="tpu_custom_call" | custom-call | tf_op jit(solution)/shard_map/pallas_call | solution.py:354

commit v5 on v3

--- a/solution.py
+++ b/solution.py
@@ -36,7 +36,7 @@
 STEPS_OUT = ((1, 1), (-1, -1), (2, -2), (-3, -3))
 PLAN = (
     ("S0", "W+1", "W-1", "S1", "S2", "Wm", "R0", "S3", "R1", "S4", "W+5", "W-5", "R2", "S5", "R3", "S6", "G1", "R4", "W2", "F", "R5", "G3", "R6", "W6", "G2", "G0", "V", "D3", "D1", "D2", "D0"),
-    ("S0", "S1", "S2", "R0", "S3", "R1", "S4", "R2", "S5", "R3", "S6", "G1", "R4", "F", "R5", "G3", "R6", "G2", "D3", "G0", "D1", "D2", "D0"),
+    ("S0", "S1", "S2", "R0", "S3", "R1", "S4", "R2", "S5", "R3", "S6", "G1", "R4", "F", "R5", "G3", "R6", "G2", "G0", "D3", "D1", "D2", "D0"),
 )
 
 

time: 102 us -> 101 us (level)
  the two profiles are of different devices: /device:TPU:6 before, /device:TPU:1 now
where the time goes in v5:
time: 101 us
  Pallas kernels  101 us (100%)
    pallas_call x1, Pallas kernels, body(): pl.pallas_call(kernel, out_shape=(jax.ShapeDtypeStruct((rows, width), BF1...  98.9 us
    pallas_call x1, Pallas kernels, body(): pl.pallas_call(finish, grid=(2,), out_shape=jax.ShapeDtypeStruct(hidden.s...  2.15 us

profile of v5, /device:TPU:1, one launch (start us, length us, event | category | flops | bytes accessed | tf_op | source)
XLA Modules:
  0.0 101.1 jit_solution(12546370058622055604)
XLA Ops:
  0.0 98.9 %shard_map.73 = (bf16[64,4096]{1,0:T(8,128)(2,1)}, bf16[64,128]{1,0:T(8,128)(2,1)}, bf16[4,8,4096]{2,1,0:T(8,128)(2,1)}) custom-call(bf16[1,64,4096]{2,1,0:T(8,128)(2,1)} %hid.1, s32[2,1,8,64]{3,2,1,0:T(8,128)} %bitcast.2, f32[2,1,8,64]{3,2,1,0:T(8,128)} %bitcast.3, bf16[1,4096]{1,0:T(2,128)(2,1)} %gain.1, bf16[1,4096,128]{2,1,0:T(8,128)(2,1)} %wg.1, ...), custom_call_target="tpu_custom_call" | custom-call | tf_op jit(solution)/shard_map/pallas_call | solution.py:306
  98.9 2.1 %shard_map.74 = bf16[1,64,4096]{2,1,0:T(8,128)(2,1)} custom-call(bf16[64,4096]{1,0:T(8,128)(2,1)} %get-tuple-element.8.x_ref, bf16[64,128]{1,0:T(8,128)(2,1)} %get-tuple-element.9.w_ref, bf16[4,8,4096]{2,1,0:T(8,128)(2,1)} %get-tuple-element.10.r_ref), custom_call_target="tpu_custom_call" | custom-call | tf_op jit(solution)/shard_map/pallas_call | solution.py:345
